TPU v7x, 256 devices: a whole 4x4x8 slice. The times are simulated.
256 devices in a mesh: ctx: 16 (over y, x), exp: 16 (over z, core).
Axes of the slice: x: 4, y: 4, z: 8, core: 2. Of those that a mesh axis runs over, the one named last changes fastest.
Arguments:
- tokens: bfloat16 [2048, 4096], P('ctx', 'exp'), may hold values from -6 to 6
- input_weight: bfloat16 [4096, 8192], P('ctx', 'exp'), may hold values from -0.09375 to 0.09375
- gate_weight: bfloat16 [4096, 8192], P('ctx', 'exp'), may hold values from -0.09375 to 0.09375
- conv_weight: float32 [4, 8192], P(None, 'exp'), may hold values from -3 to 3
- conv_bias: float32 [8192], P('exp'), may hold values from -3 to 3
- state_weight: bfloat16 [8192, 32], P('exp'), may hold values from -0.0078125 to 0.0078125
- step_size: float32 [2048, 8192], P('ctx', 'exp'), may hold values from 0 to 1, as said below
- skip_gain: float32 [8192], P('exp'), may hold values from 0.5 to 2
- output_weight: bfloat16 [8192, 4096], P('exp', 'ctx'), may hold values from -0.0625 to 0.0625
- norm_gain: float32 [4096], replicated, may hold values from 0.1 to 1.9
- router_weight: bfloat16 [4096, 16], replicated, may hold values from -0.09375 to 0.09375
- expert_gate: bfloat16 [16, 7168, 4096], P('exp', 'ctx'), may hold values from -0.09375 to 0.09375
- expert_up: bfloat16 [16, 7168, 4096], P('exp', 'ctx'), may hold values from -0.09375 to 0.09375
- expert_down: bfloat16 [16, 7168, 4096], P('exp', 'ctx'), may hold values from -0.0625 to 0.0625
- expert_ids: int32 [2048, 2], P(('ctx', 'exp')), may hold values from 0 to 15, all different within a row; in each aligned block of 8 rows (0 to 7, 8 to 15, ...) at most 2 rows name the same one
Outputs:
- layer_out: bfloat16 [2048, 4096], P(('ctx', 'exp'))
Inputs may be any that keep to these rules, and one draw needn't show every extreme that they name: `expert_ids`: each token names 2 different experts; in each aligned block of 8 tokens no expert is named by more than 2 tokens. `step_size`: a positive rate for each token and channel.
All inputs are finite; a program needn't handle non-finite values.
Results may differ from a plain program's by a relative error of at most 0.028.
Values may be sent and summed in bfloat16 or wider, within the bound.
A program may use at most 128 MiB of HBM per device.

v0:
```python
import jax
import jax.numpy as jnp
from jax import lax
from jax.sharding import PartitionSpec as P

STATE = 16
CONV = 4
TOP = 2
CAP = 2
precise = lax.Precision.HIGHEST


def shifted(shard, axis, by):
    devices = lax.axis_size(axis)
    pairs = [(i, i + by) for i in range(devices) if 0 <= i + by < devices]
    return lax.ppermute(shard, axis, pairs)


def causal_part(scores, decay_block, input_block):
    length = decay_block.shape[0]
    causal = (jnp.arange(length)[:, None] >= jnp.arange(length)[None, :])[:, :, None]
    distance = decay_block[:, None, :] - decay_block[None, :, :]
    weight = jnp.where(causal, jnp.exp(-jnp.where(causal, distance, 0.0)), 0.0)
    return jnp.einsum("ts,tsc,sc->tc", scores, weight, input_block, precision=precise)


def local(
    tokens,
    input_weight,
    gate_weight,
    conv_weight,
    conv_bias,
    state_weight,
    step_size,
    skip_gain,
    output_weight,
    norm_gain,
    router_weight,
    expert_gate,
    expert_up,
    expert_down,
    expert_ids,
):
    whole_stretch = lax.all_gather(tokens, "exp", axis=1, tiled=True)
    stretch_rows = whole_stretch.shape[0]
    inner_width = input_weight.shape[1]
    inner_x = jnp.dot(
        whole_stretch,
        lax.all_gather(input_weight, "ctx", axis=0, tiled=True),
        preferred_element_type=jnp.float32,
    )
    inner_z = jnp.dot(
        whole_stretch,
        lax.all_gather(gate_weight, "ctx", axis=0, tiled=True),
        preferred_element_type=jnp.float32,
    )
    inner_x = inner_x.astype(jnp.bfloat16)
    inner_z = inner_z.astype(jnp.bfloat16)
    earlier_rows = shifted(inner_x[stretch_rows - (CONV - 1) :], "ctx", 1)
    extended = jnp.concatenate([earlier_rows, inner_x], 0).astype(jnp.float32)
    filtered = jnp.broadcast_to(conv_bias[None, :], (stretch_rows, inner_width))
    for offset in range(CONV):
        filtered = (
            filtered + conv_weight[offset][None, :] * extended[offset : offset + stretch_rows]
        )
    mixer_in = jax.nn.silu(filtered).astype(jnp.bfloat16)
    mixer_wide = mixer_in.astype(jnp.float32)
    projections = lax.psum(
        jnp.dot(mixer_in, state_weight, preferred_element_type=jnp.float32), "exp"
    )
    input_gain = projections[:, :STATE]
    readout = projections[:, STATE:]
    cumulative = jnp.cumsum(step_size, 0)
    scores = jnp.dot(readout, input_gain.T, precision=precise)
    block_width = 128
    block_count = inner_width // block_width
    decay_blocks = cumulative.reshape(stretch_rows, block_count, block_width).transpose(1, 0, 2)
    incoming_slabs = mixer_wide.reshape(stretch_rows, block_count, block_width).transpose(1, 0, 2)
    inside = lax.map(
        lambda paired: causal_part(scores, paired[0], paired[1]), (decay_blocks, incoming_slabs)
    )
    inside = inside.transpose(1, 0, 2).reshape(stretch_rows, inner_width)
    total_decay = cumulative[stretch_rows - 1]
    tail_weight = jnp.exp(-(total_decay[None, :] - cumulative)) * mixer_wide
    local_end = jnp.dot(tail_weight.T, input_gain, precision=precise)
    stretch_keep = jnp.exp(-total_decay)

    def relay_step(turn_index, received):
        leaving = stretch_keep[:, None] * received + local_end
        return shifted(leaving, "ctx", 1)

    entering = lax.fori_loop(0, lax.axis_size("ctx") - 1, relay_step, jnp.zeros_like(local_end))
    carried = jnp.exp(-cumulative) * jnp.dot(readout, entering.T, precision=precise)
    mixed_state = (inside + carried + skip_gain[None, :] * mixer_wide) * jax.nn.silu(
        inner_z.astype(jnp.float32)
    )
    blender_result = mixed_state.astype(jnp.bfloat16)
    row_count = expert_ids.shape[0]
    start_row = lax.axis_index("exp") * row_count
    own_tokens = lax.dynamic_slice_in_dim(whole_stretch, start_row, row_count, 0)
    out_whole = lax.all_gather(output_weight, "ctx", axis=1, tiled=True)
    projected = lax.psum_scatter(
        jnp.dot(blender_result, out_whole, preferred_element_type=jnp.float32).astype(jnp.bfloat16),
        "exp",
        scatter_dimension=0,
        tiled=True,
    ).astype(jnp.float32)
    residual = (own_tokens.astype(jnp.float32) + projected).astype(jnp.bfloat16)
    stream = residual.astype(jnp.float32)
    normed = (
        stream
        * lax.rsqrt(jnp.mean(stream * stream, -1, keepdims=True) + 1e-05)
        * norm_gain[None, :]
    ).astype(jnp.bfloat16)
    logits = jnp.dot(normed, router_weight, preferred_element_type=jnp.float32)
    experts = router_weight.shape[1]
    expert_range = jnp.arange(experts, dtype=jnp.int32)
    chosen = expert_ids[:, :, None] == expert_range[None, None, :]
    selected_entry = jnp.sum(jnp.where(chosen, logits[:, None, :], 0.0), -1)
    shares = jax.nn.sigmoid(selected_entry - selected_entry[:, ::-1])
    flat_hits = chosen.reshape(row_count * TOP, experts).astype(jnp.int32)
    earlier_hits = jnp.cumsum(flat_hits, 0) - flat_hits
    slot_index = jnp.sum(earlier_hits * flat_hits, -1)
    target = expert_ids.reshape(-1) * CAP + slot_index
    placed = target[:, None] == jnp.arange(experts * CAP, dtype=jnp.int32)[None, :]
    placed = placed.reshape(row_count, TOP, experts * CAP)
    selector = jnp.any(placed, 1).astype(jnp.bfloat16)
    outgoing = lax.dot_general(
        selector, normed, (((0,), (0,)), ((), ())), preferred_element_type=jnp.float32
    ).astype(jnp.bfloat16)
    outgoing = outgoing.reshape(experts, CAP, -1)
    arrived = lax.all_to_all(outgoing, "exp", split_axis=0, concat_axis=0, tiled=True)
    arrived = arrived.reshape(-1, arrived.shape[2])
    gate_part = expert_gate[0]
    up_part = expert_up[0]
    down_part = expert_down[0]
    shard_rows = lax.all_gather(arrived, "ctx", axis=0, tiled=True)
    gate_value = lax.dot_general(
        shard_rows, gate_part, (((1,), (1,)), ((), ())), preferred_element_type=jnp.float32
    )
    up_value = lax.dot_general(
        shard_rows, up_part, (((1,), (1,)), ((), ())), preferred_element_type=jnp.float32
    )
    hidden = (jax.nn.silu(gate_value) * up_value).astype(jnp.bfloat16)
    partial_out = jnp.dot(hidden, down_part, preferred_element_type=jnp.float32)
    finished = lax.psum_scatter(
        partial_out.astype(jnp.bfloat16), "ctx", scatter_dimension=0, tiled=True
    )
    returned = lax.all_to_all(
        finished.reshape(experts, CAP, -1), "exp", split_axis=0, concat_axis=0, tiled=True
    )
    returned = returned.reshape(experts * CAP, -1).astype(jnp.float32)
    combine = jnp.sum(jnp.where(placed, shares[:, :, None], 0.0), 1)
    moe_out = jnp.dot(combine, returned, precision=precise)
    return (stream + moe_out).astype(jnp.bfloat16)


def solution(mesh):
    in_specs = (
        P("ctx", "exp"),
        P("ctx", "exp"),
        P("ctx", "exp"),
        P(None, "exp"),
        P("exp"),
        P("exp", None),
        P("ctx", "exp"),
        P("exp"),
        P("exp", "ctx"),
        P(),
        P(),
        P("exp", "ctx", None),
        P("exp", "ctx", None),
        P("exp", "ctx", None),
        P(("ctx", "exp"), None),
    )
    out_specs = P(("ctx", "exp"), None)
    return jax.shard_map(local, mesh=mesh, in_specs=in_specs, out_specs=out_specs, check_vma=False)
```

profile of v0, /device:TPU:1, one launch (start us, length us, event | category | flops | bytes accessed | tf_op | source)
XLA Modules:
  0.0 636.4 jit_solution(2759990935749958650)
XLA Ops:
  11.5 39.5 %all-gather.6.cloned.1.call-done = bf16[128,4096]{1,0:T(8,128)(2,1)} async-done(((bf16[128,256]{1,0:T(8,128)(2,1)}), bf16[128,4096]{1,0:T(8,128)(2,1)}) %all-gather.6.cloned.1.call-update) | async-done | bytes 1048592 | tf_op jit(solution)/shard_map/all_gather | solution.py:44
  51.0 57.7 %all-gather.8.cloned.1.call-done = bf16[4096,512]{1,0:T(8,128)(2,1)} async-done(((bf16[256,512]{1,0:T(8,128)(2,1)}), bf16[4096,512]{1,0:T(8,128)(2,1)}) %all-gather.8.cloned.1.call-update) | async-done | bytes 4194320 | tf_op jit(solution)/shard_map/all_gather | solution.py:49
  115.1 52.4 %all-gather.10.cloned.1.call-done = bf16[4096,512]{1,0:T(8,128)(2,1)} async-done(((bf16[256,512]{1,0:T(8,128)(2,1)}), bf16[4096,512]{1,0:T(8,128)(2,1)}) %all-gather.10.cloned.1.call-update) | async-done | bytes 4194320 | tf_op jit(solution)/shard_map/all_gather | solution.py:54
  170.7 46.7 %psum.7 = f32[128,32]{0,1:T(8,128)S(1)} all-reduce(f32[128,32]{0,1:T(8,128)S(1)} %fusion.54), channel_id=1, replica_groups=mesh['ctx'=16,'exp'=16] {'exp'}, use_global_device_ids=true, to_apply=%region_1.2 | all-reduce | flops 4096 | bytes 32768 | tf_op jit(solution)/shard_map/psum | solution.py:68
  218.1 39.1 %while.20 = (s32[]{:T(128)}, f32[4,128,128]{2,1,0:T(8,128)S(1)}, f32[4,128,128]{2,1,0:T(8,128)S(1)}, f32[4,128,128]{2,1,0:T(8,128)S(1)}, f32[128,128]{1,0:T(8,128)S(1)}, /*index=5*/s32[]{:T(128)}) while((s32[]{:T(128)}, f32[4,128,128]{2,1,0:T(8,128)S(1)}, f32[4,128,128]{2,1,0:T(8,128)S(1)}, f32[4,128,128]{2,1,0:T(8,128)S(1)}, ...), condition=%wide.region_3.4_spmd, body=%wide.region_2.3_spmd.sunk | while | flops 35667968 | bytes 688205 | solution.py:79
  218.1 9.7 %fusion.87 = f32[128,1,128]{2,1,0:T(1,128)S(1)} fusion(f32[128,128,1]{1,2,0:T(1,128)S(1)} %bitcast.88, f32[128,128]{1,0:T(8,128)S(1)} %get-tuple-element.140, f32[128,128]{1,0:T(8,128)S(1)} %get-tuple-element.141, pred[128,128]{1,0:T(8,128)(4,1)S(1)} %iota_compare_fusion.5), kind=kOutput, calls=%fused_computation.clone.1 | convolution fusion | flops 35651584 | bytes 278528 | tf_op jit(solution)/shard_map/while/body/eval_jaxpr/ts,tsc,sc->tc/dot_general | solution.py:24
  227.9 9.7 %fusion.87 = f32[128,1,128]{2,1,0:T(1,128)S(1)} fusion(f32[128,128,1]{1,2,0:T(1,128)S(1)} %bitcast.88, f32[128,128]{1,0:T(8,128)S(1)} %get-tuple-element.140, f32[128,128]{1,0:T(8,128)S(1)} %get-tuple-element.141, pred[128,128]{1,0:T(8,128)(4,1)S(1)} %iota_compare_fusion.5), kind=kOutput, calls=%fused_computation.clone.1 | convolution fusion | flops 35651584 | bytes 278528 | tf_op jit(solution)/shard_map/while/body/eval_jaxpr/ts,tsc,sc->tc/dot_general | solution.py:24
  237.6 9.7 %fusion.87 = f32[128,1,128]{2,1,0:T(1,128)S(1)} fusion(f32[128,128,1]{1,2,0:T(1,128)S(1)} %bitcast.88, f32[128,128]{1,0:T(8,128)S(1)} %get-tuple-element.140, f32[128,128]{1,0:T(8,128)S(1)} %get-tuple-element.141, pred[128,128]{1,0:T(8,128)(4,1)S(1)} %iota_compare_fusion.5), kind=kOutput, calls=%fused_computation.clone.1 | convolution fusion | flops 35651584 | bytes 278528 | tf_op jit(solution)/shard_map/while/body/eval_jaxpr/ts,tsc,sc->tc/dot_general | solution.py:24
  247.4 9.7 %fusion.87 = f32[128,1,128]{2,1,0:T(1,128)S(1)} fusion(f32[128,128,1]{1,2,0:T(1,128)S(1)} %bitcast.88, f32[128,128]{1,0:T(8,128)S(1)} %get-tuple-element.140, f32[128,128]{1,0:T(8,128)S(1)} %get-tuple-element.141, pred[128,128]{1,0:T(8,128)(4,1)S(1)} %iota_compare_fusion.5), kind=kOutput, calls=%fused_computation.clone.1 | convolution fusion | flops 35651584 | bytes 278528 | tf_op jit(solution)/shard_map/while/body/eval_jaxpr/ts,tsc,sc->tc/dot_general | solution.py:24
  257.1 90.6 %while.21 = (s32[]{:T(128)}, f32[512,16]{0,1:T(8,128)S(1)}, f32[512]{0:T(512)S(1)}, f32[512,16]{0,1:T(8,128)S(1)}, s32[]{:T(128)}) while((s32[]{:T(128)}, f32[512,16]{0,1:T(8,128)S(1)}, f32[512]{0:T(512)S(1)}, f32[512,16]{0,1:T(8,128)S(1)}, s32[]{:T(128)}) %tuple.40), condition=%wide.region_5.6_spmd, body=%wide.region_4.5_spmd.sunk | while | flops 16386 | bytes 231525 | solution.py:92
  280.0 5.8 collective-permute-start
  293.5 5.8 collective-permute-start
  300.3 5.8 collective-permute-start
  307.1 5.8 collective-permute-start
  313.8 5.8 collective-permute-start
  320.6 5.8 collective-permute-start
  340.9 5.8 collective-permute-start
  352.9 81.0 %reduce-scatter.3.cloned.1.call-done = bf16[8,4096]{1,0:T(8,128)(2,1)} async-done(((bf16[128,4096]{1,0:T(8,128)(2,1)}), bf16[8,4096]{1,0:T(8,128)(2,1)}) %reduce-scatter.3.cloned.1.call-update) | async-done | bytes 65552 | tf_op jit(solution)/shard_map/reduce_scatter | solution.py:102
  435.4 19.1 %all_to_all.10 = bf16[16,2,4096]{2,1,0:T(2,128)(2,1)S(1)} all-to-all(bf16[16,2,4096]{2,1,0:T(2,128)(2,1)S(1)} %reshape.74), channel_id=1, replica_groups=mesh['ctx'=16,'exp'=16] {'exp'}, dimensions={0} | all-to-all | bytes 524288 | tf_op jit(solution)/shard_map/all_to_all | solution.py:132
  455.5 53.0 %all-gather.14.cloned.1.call-done = bf16[512,4096]{1,0:T(8,128)(2,1)} async-done(((bf16[32,4096]{1,0:T(8,128)(2,1)}), bf16[512,4096]{1,0:T(8,128)(2,1)}) %all-gather.14.cloned.1.call-update) | async-done | bytes 4194320 | tf_op jit(solution)/shard_map/all_gather | solution.py:137
  513.9 10.8 %convolution_convert_fusion = bf16[512,4096]{1,0:T(8,128)(2,1)} fusion(bf16[1,448,4096]{2,1,0:T(8,128)(2,1)} %param.32, bf16[512,4096]{1,0:T(8,128)(2,1)} %all-gather.14.cloned.1.call-done, bf16[1,448,4096]{2,1,0:T(8,128)(2,1)} %param.31, f32[512,448]{0,1:T(8,128)S(1)} %fusion.18), kind=kOutput, calls=%fused_computation.19 | convolution fusion | flops 3761569792 | bytes 16646144 | tf_op jit(solution)/shard_map/dot_general | solution.py:145
  524.7 81.0 %reduce-scatter.5.cloned.1.call-done = bf16[32,4096]{1,0:T(8,128)(2,1)} async-done(((bf16[512,4096]{1,0:T(8,128)(2,1)}), bf16[32,4096]{1,0:T(8,128)(2,1)}) %reduce-scatter.5.cloned.1.call-update) | async-done | bytes 262160 | tf_op jit(solution)/shard_map/reduce_scatter | solution.py:146
  607.5 9.3 %all-to-all-start.1 = ((bf16[16,2,4096]{2,1,0:T(2,128)(2,1)}), bf16[16,2,4096]{2,1,0:T(2,128)(2,1)S(1)}, u32[]{:S(2)}, u32[]{:S(2)}) async-start(bf16[16,2,4096]{2,1,0:T(2,128)(2,1)} %reshape.76), calls=%async_computation.3 | async-start | bytes 524288 | tf_op jit(solution)/shard_map/all_to_all | solution.py:149
  617.3 11.2 %all-to-all-done.1 = bf16[16,2,4096]{2,1,0:T(2,128)(2,1)S(1)} async-done(((bf16[16,2,4096]{2,1,0:T(2,128)(2,1)}), bf16[16,2,4096]{2,1,0:T(2,128)(2,1)S(1)}, u32[]{:S(2)}, u32[]{:S(2)}) %all-to-all-start.1) | async-done | bytes 262176 | tf_op jit(solution)/shard_map/all_to_all | solution.py:149
  (121 shorter events, 81.6 us)
Async XLA Ops:
  6.5 44.5 %all-gather.6.cloned.1.call-start = ((), (), s32[]{:S(2)}) async-start(), calls=%async_computation.4 | async-start | bytes 1114112 | tf_op jit(solution)/shard_map/all_gather | solution.py:44
  7.3 101.4 %all-gather.8.cloned.1.call-start = ((), (), s32[]{:S(2)}) async-start(), calls=%async_computation.5 | async-start | bytes 4456448 | tf_op jit(solution)/shard_map/all_gather | solution.py:49
  8.0 159.4 %all-gather.10.cloned.1.call-start = ((), (), s32[]{:S(2)}) async-start(), calls=%async_computation.6 | async-start | bytes 4456448 | tf_op jit(solution)/shard_map/all_gather | solution.py:54
  8.7 339.5 %all-gather.12.cloned.1.call-start = ((), (), s32[]{:S(2)}) async-start(), calls=%async_computation.7 | async-start | bytes 4456448 | tf_op jit(solution)/shard_map/all_gather | solution.py:101
  9.3 424.6 %reduce-scatter.3.cloned.1.call-start = ((), (), s32[]{:S(2)}) async-start(), calls=%async_computation.8 | async-start | bytes 1114112 | tf_op jit(solution)/shard_map/reduce_scatter | solution.py:102
  112.0 58.4 %collective-permute-start.1 = (bf16[3,512]{1,0:T(4,128)(2,1)S(1)}, bf16[3,512]{1,0:T(4,128)(2,1)S(1)}, u32[]{:S(2)}, u32[]{:S(2)}) collective-permute-start(bf16[3,512]{1,0:T(4,128)(2,1)S(1)} %slice.48), channel_id=1, source_target_pairs={{0,16},{16,32},{32,48},{48,64},{64,80},{80,96},{96,112},{112,128},... | collective-permute-start | bytes 9224 | tf_op jit(solution)/shard_map/ppermute | solution.py:16
  257.2 3.7 collective-permute-start
  260.9 4.7 collective-permute-start
  265.5 4.7 collective-permute-start
  270.2 5.1 collective-permute-start
  275.3 4.7 collective-permute-start
  280.0 6.9 %collective-permute-start = (f32[512,16]{0,1:T(8,128)S(1)}, f32[512,16]{0,1:T(8,128)S(1)}, u32[]{:S(2)}, u32[]{:S(2)}) collective-permute-start(f32[512,16]{0,1:T(8,128)S(1)} %multiply_add_fusion.3), channel_id=1, source_target_pairs={{0,16},{16,32},{32,48},{48,64},{64,80},{80,96},{96,112},{112,128},... | collective-permute-start | bytes 98312 | tf_op jit(solution)/shard_map/while/body/eval_jaxpr/ppermute | solution.py:16
  286.8 6.7 %collective-permute-start = (f32[512,16]{0,1:T(8,128)S(1)}, f32[512,16]{0,1:T(8,128)S(1)}, u32[]{:S(2)}, u32[]{:S(2)}) collective-permute-start(f32[512,16]{0,1:T(8,128)S(1)} %multiply_add_fusion.3), channel_id=1, source_target_pairs={{0,16},{16,32},{32,48},{48,64},{64,80},{80,96},{96,112},{112,128},... | collective-permute-start | bytes 98312 | tf_op jit(solution)/shard_map/while/body/eval_jaxpr/ppermute | solution.py:16
  293.5 6.8 %collective-permute-start = (f32[512,16]{0,1:T(8,128)S(1)}, f32[512,16]{0,1:T(8,128)S(1)}, u32[]{:S(2)}, u32[]{:S(2)}) collective-permute-start(f32[512,16]{0,1:T(8,128)S(1)} %multiply_add_fusion.3), channel_id=1, source_target_pairs={{0,16},{16,32},{32,48},{48,64},{64,80},{80,96},{96,112},{112,128},... | collective-permute-start | bytes 98312 | tf_op jit(solution)/shard_map/while/body/eval_jaxpr/ppermute | solution.py:16
  300.3 6.8 %collective-permute-start = (f32[512,16]{0,1:T(8,128)S(1)}, f32[512,16]{0,1:T(8,128)S(1)}, u32[]{:S(2)}, u32[]{:S(2)}) collective-permute-start(f32[512,16]{0,1:T(8,128)S(1)} %multiply_add_fusion.3), channel_id=1, source_target_pairs={{0,16},{16,32},{32,48},{48,64},{64,80},{80,96},{96,112},{112,128},... | collective-permute-start | bytes 98312 | tf_op jit(solution)/shard_map/while/body/eval_jaxpr/ppermute | solution.py:16
  307.1 6.8 %collective-permute-start = (f32[512,16]{0,1:T(8,128)S(1)}, f32[512,16]{0,1:T(8,128)S(1)}, u32[]{:S(2)}, u32[]{:S(2)}) collective-permute-start(f32[512,16]{0,1:T(8,128)S(1)} %multiply_add_fusion.3), channel_id=1, source_target_pairs={{0,16},{16,32},{32,48},{48,64},{64,80},{80,96},{96,112},{112,128},... | collective-permute-start | bytes 98312 | tf_op jit(solution)/shard_map/while/body/eval_jaxpr/ppermute | solution.py:16
  313.8 6.8 %collective-permute-start = (f32[512,16]{0,1:T(8,128)S(1)}, f32[512,16]{0,1:T(8,128)S(1)}, u32[]{:S(2)}, u32[]{:S(2)}) collective-permute-start(f32[512,16]{0,1:T(8,128)S(1)} %multiply_add_fusion.3), channel_id=1, source_target_pairs={{0,16},{16,32},{32,48},{48,64},{64,80},{80,96},{96,112},{112,128},... | collective-permute-start | bytes 98312 | tf_op jit(solution)/shard_map/while/body/eval_jaxpr/ppermute | solution.py:16
  320.6 6.9 %collective-permute-start = (f32[512,16]{0,1:T(8,128)S(1)}, f32[512,16]{0,1:T(8,128)S(1)}, u32[]{:S(2)}, u32[]{:S(2)}) collective-permute-start(f32[512,16]{0,1:T(8,128)S(1)} %multiply_add_fusion.3), channel_id=1, source_target_pairs={{0,16},{16,32},{32,48},{48,64},{64,80},{80,96},{96,112},{112,128},... | collective-permute-start | bytes 98312 | tf_op jit(solution)/shard_map/while/body/eval_jaxpr/ppermute | solution.py:16
  327.6 6.6 %collective-permute-start = (f32[512,16]{0,1:T(8,128)S(1)}, f32[512,16]{0,1:T(8,128)S(1)}, u32[]{:S(2)}, u32[]{:S(2)}) collective-permute-start(f32[512,16]{0,1:T(8,128)S(1)} %multiply_add_fusion.3), channel_id=1, source_target_pairs={{0,16},{16,32},{32,48},{48,64},{64,80},{80,96},{96,112},{112,128},... | collective-permute-start | bytes 98312 | tf_op jit(solution)/shard_map/while/body/eval_jaxpr/ppermute | solution.py:16
  334.2 6.8 %collective-permute-start = (f32[512,16]{0,1:T(8,128)S(1)}, f32[512,16]{0,1:T(8,128)S(1)}, u32[]{:S(2)}, u32[]{:S(2)}) collective-permute-start(f32[512,16]{0,1:T(8,128)S(1)} %multiply_add_fusion.3), channel_id=1, source_target_pairs={{0,16},{16,32},{32,48},{48,64},{64,80},{80,96},{96,112},{112,128},... | collective-permute-start | bytes 98312 | tf_op jit(solution)/shard_map/while/body/eval_jaxpr/ppermute | solution.py:16
  340.9 6.8 %collective-permute-start = (f32[512,16]{0,1:T(8,128)S(1)}, f32[512,16]{0,1:T(8,128)S(1)}, u32[]{:S(2)}, u32[]{:S(2)}) collective-permute-start(f32[512,16]{0,1:T(8,128)S(1)} %multiply_add_fusion.3), channel_id=1, source_target_pairs={{0,16},{16,32},{32,48},{48,64},{64,80},{80,96},{96,112},{112,128},... | collective-permute-start | bytes 98312 | tf_op jit(solution)/shard_map/while/body/eval_jaxpr/ppermute | solution.py:16
  352.1 156.4 %all-gather.14.cloned.1.call-start = ((), (), s32[]{:S(2)}) async-start(), calls=%async_computation.9 | async-start | bytes 4456448 | tf_op jit(solution)/shard_map/all_gather | solution.py:137
  455.3 150.4 %reduce-scatter.5.cloned.1.call-start = ((), (), s32[]{:S(2)}) async-start(), calls=%async_computation.10 | async-start | bytes 4456448 | tf_op jit(solution)/shard_map/reduce_scatter | solution.py:146
  607.5 21.1 %all-to-all-start.1 = ((bf16[16,2,4096]{2,1,0:T(2,128)(2,1)}), bf16[16,2,4096]{2,1,0:T(2,128)(2,1)S(1)}, u32[]{:S(2)}, u32[]{:S(2)}) async-start(bf16[16,2,4096]{2,1,0:T(2,128)(2,1)} %reshape.76), calls=%async_computation.3 | async-start | bytes 524288 | tf_op jit(solution)/shard_map/all_to_all | solution.py:149
  (7 other events, 1065.3 us)
Sparse Core Ops, SparseCore 0:
  9.1 41.8 all-gather.5
  53.4 55.2 all-gather.7
  111.1 56.2 all-gather.9
  169.7 61.4 all-gather.11
  352.2 81.6 reduce-scatter.2
  455.4 53.0 all-gather.13
  524.8 80.7 reduce-scatter.4
where the time goes:
time: 637 us; the launch traced here: 636 us
  waiting for transfers between devices  394 us (62%)
  starting transfers between devices  87.9 us (14%)
  matrix products  67.4 us (11%)
  blocking collectives  65.7 us (10%)
  between operations  13.7 us (2%)
    reduce_scatter x1, waiting for transfers between devices, local(): lax.psum_scatter(jnp.dot(blender_result, out_whole, preferred_element_typ...  81 us
    reduce_scatter x1, waiting for transfers between devices, local(): lax.psum_scatter(partial_out.astype(jnp.bfloat16), 'ctx', scatter_dimensi...  81 us
    ppermute x16, starting transfers between devices, shifted(): return lax.ppermute(shard, axis, pairs)  78.2 us
    all_gather x1, waiting for transfers between devices, local(): lax.all_gather(input_weight, 'ctx', axis=0, tiled=True)  57.7 us
    all_gather x1, waiting for transfers between devices, local(): shard_rows = lax.all_gather(arrived, 'ctx', axis=0, tiled=True)  53 us
    all_gather x1, waiting for transfers between devices, local(): lax.all_gather(gate_weight, 'ctx', axis=0, tiled=True)  52.4 us
    psum x1, blocking collectives, local(): lax.psum(jnp.dot(mixer_in, state_weight, preferred_element_type=jnp.float...  46.7 us
    all_gather x1, waiting for transfers between devices, local(): whole_stretch = lax.all_gather(tokens, 'exp', axis=1, tiled=True)  39.5 us
  transfers between devices with their start and end apart: 24, of which 22 were waited for; matrix products, arithmetic and copies ran while one was open for 8% of the time, Pallas kernels for 0%

commit v1 on v0

--- a/solution.py
+++ b/solution.py
@@ -65,8 +65,9 @@
         )
     mixer_in = jax.nn.silu(filtered).astype(jnp.bfloat16)
     mixer_wide = mixer_in.astype(jnp.float32)
-    projections = lax.psum(
-        jnp.dot(mixer_in, state_weight, preferred_element_type=jnp.float32), "exp"
+    projections = jnp.sum(
+        lax.all_gather(jnp.dot(mixer_in, state_weight, preferred_element_type=jnp.float32), "exp"),
+        axis=0,
     )
     input_gain = projections[:, :STATE]
     readout = projections[:, STATE:]

time: 637 us -> 606 us (0.951)
  blocking collectives: 65.7 us -> 37.8 us
    psum x1 -> x0, blocking collectives: 46.7 us -> none  [local(): lax.psum(jnp.dot(mixer_in, state_weight, preferred_element_type=jnp.float...]
    all_gather x0 -> x1, blocking collectives: none -> 18.7 us  [local(): lax.all_gather(jnp.dot(mixer_in, state_weight, preferred_element_type=jnp...]
where the time goes in v1:
time: 606 us
  waiting for transfers between devices  391 us (65%)
  starting transfers between devices  88 us (15%)
  matrix products  67.4 us (11%)
  blocking collectives  37.8 us (6%)
  between operations  13.7 us (2%)
    reduce_scatter x1, waiting for transfers between devices, local(): lax.psum_scatter(partial_out.astype(jnp.bfloat16), 'ctx', scatter_dimensi...  80.9 us
    ppermute x16, starting transfers between devices, shifted(): return lax.ppermute(shard, axis, pairs)  78.3 us
    reduce_scatter x1, waiting for transfers between devices, local(): lax.psum_scatter(jnp.dot(blender_result, out_whole, preferred_element_typ...  77.7 us
    all_gather x1, waiting for transfers between devices, local(): lax.all_gather(input_weight, 'ctx', axis=0, tiled=True)  57.7 us
    all_gather x1, waiting for transfers between devices, local(): shard_rows = lax.all_gather(arrived, 'ctx', axis=0, tiled=True)  53.1 us
    all_gather x1, waiting for transfers between devices, local(): lax.all_gather(gate_weight, 'ctx', axis=0, tiled=True)  52.4 us
    all_gather x1, waiting for transfers between devices, local(): whole_stretch = lax.all_gather(tokens, 'exp', axis=1, tiled=True)  39.5 us
    dot_general x4, matrix products, causal_part(): jnp.einsum('ts,tsc,sc->tc', scores, weight, input_block, precision=precise)  38.7 us
  transfers between devices with their start and end apart: 24, of which 22 were waited for; matrix products, arithmetic and copies ran while one was open for 8% of the time, Pallas kernels for 0%

profile of v1, /device:TPU:1, one launch (start us, length us, event | category | flops | bytes accessed | tf_op | source)
XLA Modules:
  0.0 605.5 jit_solution(11083080969810667060)
XLA Ops:
  11.5 39.5 %all-gather.7.cloned.1.call-done = bf16[128,4096]{1,0:T(8,128)(2,1)} async-done(((bf16[128,256]{1,0:T(8,128)(2,1)}), bf16[128,4096]{1,0:T(8,128)(2,1)}) %all-gather.7.cloned.1.call-update) | async-done | bytes 1048592 | tf_op jit(solution)/shard_map/all_gather | solution.py:44
  51.0 57.7 %all-gather.9.cloned.1.call-done = bf16[4096,512]{1,0:T(8,128)(2,1)} async-done(((bf16[256,512]{1,0:T(8,128)(2,1)}), bf16[4096,512]{1,0:T(8,128)(2,1)}) %all-gather.9.cloned.1.call-update) | async-done | bytes 4194320 | tf_op jit(solution)/shard_map/all_gather | solution.py:49
  115.1 52.4 %all-gather.11.cloned.1.call-done = bf16[4096,512]{1,0:T(8,128)(2,1)} async-done(((bf16[256,512]{1,0:T(8,128)(2,1)}), bf16[4096,512]{1,0:T(8,128)(2,1)}) %all-gather.11.cloned.1.call-update) | async-done | bytes 4194320 | tf_op jit(solution)/shard_map/all_gather | solution.py:54
  170.7 18.7 %all-gather = f32[2048,32]{0,1:T(8,128)S(1)} all-gather(f32[128,32]{0,1:T(8,128)S(1)} %fusion.54), channel_id=2, replica_groups=mesh['ctx'=16,'exp'=16] {'exp'}, dimensions={0}, use_global_device_ids=true | all-gather | bytes 278528 | tf_op jit(solution)/shard_map/all_gather | solution.py:69
  190.1 39.1 %while.20 = (s32[]{:T(128)}, f32[4,128,128]{2,1,0:T(8,128)S(1)}, f32[4,128,128]{2,1,0:T(8,128)S(1)}, f32[4,128,128]{2,1,0:T(8,128)S(1)}, f32[128,128]{1,0:T(8,128)S(1)}, /*index=5*/s32[]{:T(128)}) while((s32[]{:T(128)}, f32[4,128,128]{2,1,0:T(8,128)S(1)}, f32[4,128,128]{2,1,0:T(8,128)S(1)}, f32[4,128,128]{2,1,0:T(8,128)S(1)}, ...), condition=%wide.region_3.4_spmd, body=%wide.region_2.3_spmd.sunk | while | flops 35667968 | bytes 688205 | solution.py:80
  190.2 9.7 %fusion.87 = f32[128,1,128]{2,1,0:T(1,128)S(1)} fusion(f32[128,128,1]{1,2,0:T(1,128)S(1)} %bitcast.97, f32[128,128]{1,0:T(8,128)S(1)} %get-tuple-element.138, f32[128,128]{1,0:T(8,128)S(1)} %get-tuple-element.139, pred[128,128]{1,0:T(8,128)(4,1)S(1)} %iota_compare_fusion.5), kind=kOutput, calls=%fused_computation.clone.1 | convolution fusion | flops 35651584 | bytes 278528 | tf_op jit(solution)/shard_map/while/body/eval_jaxpr/ts,tsc,sc->tc/dot_general | solution.py:24
  200.0 9.7 %fusion.87 = f32[128,1,128]{2,1,0:T(1,128)S(1)} fusion(f32[128,128,1]{1,2,0:T(1,128)S(1)} %bitcast.97, f32[128,128]{1,0:T(8,128)S(1)} %get-tuple-element.138, f32[128,128]{1,0:T(8,128)S(1)} %get-tuple-element.139, pred[128,128]{1,0:T(8,128)(4,1)S(1)} %iota_compare_fusion.5), kind=kOutput, calls=%fused_computation.clone.1 | convolution fusion | flops 35651584 | bytes 278528 | tf_op jit(solution)/shard_map/while/body/eval_jaxpr/ts,tsc,sc->tc/dot_general | solution.py:24
  209.7 9.7 %fusion.87 = f32[128,1,128]{2,1,0:T(1,128)S(1)} fusion(f32[128,128,1]{1,2,0:T(1,128)S(1)} %bitcast.97, f32[128,128]{1,0:T(8,128)S(1)} %get-tuple-element.138, f32[128,128]{1,0:T(8,128)S(1)} %get-tuple-element.139, pred[128,128]{1,0:T(8,128)(4,1)S(1)} %iota_compare_fusion.5), kind=kOutput, calls=%fused_computation.clone.1 | convolution fusion | flops 35651584 | bytes 278528 | tf_op jit(solution)/shard_map/while/body/eval_jaxpr/ts,tsc,sc->tc/dot_general | solution.py:24
  219.5 9.7 %fusion.87 = f32[128,1,128]{2,1,0:T(1,128)S(1)} fusion(f32[128,128,1]{1,2,0:T(1,128)S(1)} %bitcast.97, f32[128,128]{1,0:T(8,128)S(1)} %get-tuple-element.138, f32[128,128]{1,0:T(8,128)S(1)} %get-tuple-element.139, pred[128,128]{1,0:T(8,128)(4,1)S(1)} %iota_compare_fusion.5), kind=kOutput, calls=%fused_computation.clone.1 | convolution fusion | flops 35651584 | bytes 278528 | tf_op jit(solution)/shard_map/while/body/eval_jaxpr/ts,tsc,sc->tc/dot_general | solution.py:24
  229.2 90.8 %while.21 = (s32[]{:T(128)}, f32[512,16]{0,1:T(8,128)S(1)}, f32[512]{0:T(512)S(1)}, f32[512,16]{0,1:T(8,128)S(1)}, s32[]{:T(128)}) while((s32[]{:T(128)}, f32[512,16]{0,1:T(8,128)S(1)}, f32[512]{0:T(512)S(1)}, f32[512,16]{0,1:T(8,128)S(1)}, s32[]{:T(128)}) %tuple.39), condition=%wide.region_5.6_spmd, body=%wide.region_4.5_spmd.sunk | while | flops 16386 | bytes 231525 | solution.py:93
  252.1 5.8 collective-permute-start
  258.9 5.8 collective-permute-start
  265.6 5.8 collective-permute-start
  279.2 5.8 collective-permute-start
  285.9 5.8 collective-permute-start
  292.7 5.8 collective-permute-start
  299.5 5.8 collective-permute-start
  325.2 77.7 %reduce-scatter.3.cloned.1.call-done = bf16[8,4096]{1,0:T(8,128)(2,1)} async-done(((bf16[128,4096]{1,0:T(8,128)(2,1)}), bf16[8,4096]{1,0:T(8,128)(2,1)}) %reduce-scatter.3.cloned.1.call-update) | async-done | bytes 65552 | tf_op jit(solution)/shard_map/reduce_scatter | solution.py:103
  404.4 19.1 %all_to_all.10 = bf16[16,2,4096]{2,1,0:T(2,128)(2,1)S(1)} all-to-all(bf16[16,2,4096]{2,1,0:T(2,128)(2,1)S(1)} %reshape.74), channel_id=1, replica_groups=mesh['ctx'=16,'exp'=16] {'exp'}, dimensions={0} | all-to-all | bytes 524288 | tf_op jit(solution)/shard_map/all_to_all | solution.py:133
  424.6 53.1 %all-gather.15.cloned.1.call-done = bf16[512,4096]{1,0:T(8,128)(2,1)} async-done(((bf16[32,4096]{1,0:T(8,128)(2,1)}), bf16[512,4096]{1,0:T(8,128)(2,1)}) %all-gather.15.cloned.1.call-update) | async-done | bytes 4194320 | tf_op jit(solution)/shard_map/all_gather | solution.py:138
  483.1 10.8 %convolution_convert_fusion = bf16[512,4096]{1,0:T(8,128)(2,1)} fusion(bf16[1,448,4096]{2,1,0:T(8,128)(2,1)} %param.32, bf16[512,4096]{1,0:T(8,128)(2,1)} %all-gather.15.cloned.1.call-done, bf16[1,448,4096]{2,1,0:T(8,128)(2,1)} %param.31, f32[512,448]{0,1:T(8,128)S(1)} %fusion.18), kind=kOutput, calls=%fused_computation.19 | convolution fusion | flops 3761569792 | bytes 16646144 | tf_op jit(solution)/shard_map/dot_general | solution.py:146
  493.9 80.9 %reduce-scatter.5.cloned.1.call-done = bf16[32,4096]{1,0:T(8,128)(2,1)} async-done(((bf16[512,4096]{1,0:T(8,128)(2,1)}), bf16[32,4096]{1,0:T(8,128)(2,1)}) %reduce-scatter.5.cloned.1.call-update) | async-done | bytes 262160 | tf_op jit(solution)/shard_map/reduce_scatter | solution.py:147
  576.6 9.4 %all-to-all-start.1 = ((bf16[16,2,4096]{2,1,0:T(2,128)(2,1)}), bf16[16,2,4096]{2,1,0:T(2,128)(2,1)S(1)}, u32[]{:S(2)}, u32[]{:S(2)}) async-start(bf16[16,2,4096]{2,1,0:T(2,128)(2,1)} %reshape.76), calls=%async_computation.3 | async-start | bytes 524288 | tf_op jit(solution)/shard_map/all_to_all | solution.py:150
  586.5 11.2 %all-to-all-done.1 = bf16[16,2,4096]{2,1,0:T(2,128)(2,1)S(1)} async-done(((bf16[16,2,4096]{2,1,0:T(2,128)(2,1)}), bf16[16,2,4096]{2,1,0:T(2,128)(2,1)S(1)}, u32[]{:S(2)}, u32[]{:S(2)}) %all-to-all-start.1) | async-done | bytes 262176 | tf_op jit(solution)/shard_map/all_to_all | solution.py:150
  (124 shorter events, 82.0 us)
Async XLA Ops:
  6.5 44.5 %all-gather.7.cloned.1.call-start = ((), (), s32[]{:S(2)}) async-start(), calls=%async_computation.4 | async-start | bytes 1114112 | tf_op jit(solution)/shard_map/all_gather | solution.py:44
  7.3 101.4 %all-gather.9.cloned.1.call-start = ((), (), s32[]{:S(2)}) async-start(), calls=%async_computation.5 | async-start | bytes 4456448 | tf_op jit(solution)/shard_map/all_gather | solution.py:49
  8.0 159.4 %all-gather.11.cloned.1.call-start = ((), (), s32[]{:S(2)}) async-start(), calls=%async_computation.6 | async-start | bytes 4456448 | tf_op jit(solution)/shard_map/all_gather | solution.py:54
  8.7 311.8 %all-gather.13.cloned.1.call-start = ((), (), s32[]{:S(2)}) async-start(), calls=%async_computation.7 | async-start | bytes 4456448 | tf_op jit(solution)/shard_map/all_gather | solution.py:102
  9.3 393.6 %reduce-scatter.3.cloned.1.call-start = ((), (), s32[]{:S(2)}) async-start(), calls=%async_computation.8 | async-start | bytes 1114112 | tf_op jit(solution)/shard_map/reduce_scatter | solution.py:103
  112.0 58.4 %collective-permute-start.1 = (bf16[3,512]{1,0:T(4,128)(2,1)S(1)}, bf16[3,512]{1,0:T(4,128)(2,1)S(1)}, u32[]{:S(2)}, u32[]{:S(2)}) collective-permute-start(bf16[3,512]{1,0:T(4,128)(2,1)S(1)} %slice.48), channel_id=1, source_target_pairs={{0,16},{16,32},{32,48},{48,64},{64,80},{80,96},{96,112},{112,128},... | collective-permute-start | bytes 9224 | tf_op jit(solution)/shard_map/ppermute | solution.py:16
  229.2 4.1 collective-permute-start
  233.4 4.7 collective-permute-start
  238.0 4.7 collective-permute-start
  242.7 4.7 collective-permute-start
  247.3 4.7 collective-permute-start
  252.1 6.8 %collective-permute-start = (f32[512,16]{0,1:T(8,128)S(1)}, f32[512,16]{0,1:T(8,128)S(1)}, u32[]{:S(2)}, u32[]{:S(2)}) collective-permute-start(f32[512,16]{0,1:T(8,128)S(1)} %multiply_add_fusion.3), channel_id=1, source_target_pairs={{0,16},{16,32},{32,48},{48,64},{64,80},{80,96},{96,112},{112,128},... | collective-permute-start | bytes 98312 | tf_op jit(solution)/shard_map/while/body/eval_jaxpr/ppermute | solution.py:16
  258.9 6.8 %collective-permute-start = (f32[512,16]{0,1:T(8,128)S(1)}, f32[512,16]{0,1:T(8,128)S(1)}, u32[]{:S(2)}, u32[]{:S(2)}) collective-permute-start(f32[512,16]{0,1:T(8,128)S(1)} %multiply_add_fusion.3), channel_id=1, source_target_pairs={{0,16},{16,32},{32,48},{48,64},{64,80},{80,96},{96,112},{112,128},... | collective-permute-start | bytes 98312 | tf_op jit(solution)/shard_map/while/body/eval_jaxpr/ppermute | solution.py:16
  265.6 6.8 %collective-permute-start = (f32[512,16]{0,1:T(8,128)S(1)}, f32[512,16]{0,1:T(8,128)S(1)}, u32[]{:S(2)}, u32[]{:S(2)}) collective-permute-start(f32[512,16]{0,1:T(8,128)S(1)} %multiply_add_fusion.3), channel_id=1, source_target_pairs={{0,16},{16,32},{32,48},{48,64},{64,80},{80,96},{96,112},{112,128},... | collective-permute-start | bytes 98312 | tf_op jit(solution)/shard_map/while/body/eval_jaxpr/ppermute | solution.py:16
  272.5 6.7 %collective-permute-start = (f32[512,16]{0,1:T(8,128)S(1)}, f32[512,16]{0,1:T(8,128)S(1)}, u32[]{:S(2)}, u32[]{:S(2)}) collective-permute-start(f32[512,16]{0,1:T(8,128)S(1)} %multiply_add_fusion.3), channel_id=1, source_target_pairs={{0,16},{16,32},{32,48},{48,64},{64,80},{80,96},{96,112},{112,128},... | collective-permute-start | bytes 98312 | tf_op jit(solution)/shard_map/while/body/eval_jaxpr/ppermute | solution.py:16
  279.2 6.8 %collective-permute-start = (f32[512,16]{0,1:T(8,128)S(1)}, f32[512,16]{0,1:T(8,128)S(1)}, u32[]{:S(2)}, u32[]{:S(2)}) collective-permute-start(f32[512,16]{0,1:T(8,128)S(1)} %multiply_add_fusion.3), channel_id=1, source_target_pairs={{0,16},{16,32},{32,48},{48,64},{64,80},{80,96},{96,112},{112,128},... | collective-permute-start | bytes 98312 | tf_op jit(solution)/shard_map/while/body/eval_jaxpr/ppermute | solution.py:16
  285.9 6.8 %collective-permute-start = (f32[512,16]{0,1:T(8,128)S(1)}, f32[512,16]{0,1:T(8,128)S(1)}, u32[]{:S(2)}, u32[]{:S(2)}) collective-permute-start(f32[512,16]{0,1:T(8,128)S(1)} %multiply_add_fusion.3), channel_id=1, source_target_pairs={{0,16},{16,32},{32,48},{48,64},{64,80},{80,96},{96,112},{112,128},... | collective-permute-start | bytes 98312 | tf_op jit(solution)/shard_map/while/body/eval_jaxpr/ppermute | solution.py:16
  292.7 6.8 %collective-permute-start = (f32[512,16]{0,1:T(8,128)S(1)}, f32[512,16]{0,1:T(8,128)S(1)}, u32[]{:S(2)}, u32[]{:S(2)}) collective-permute-start(f32[512,16]{0,1:T(8,128)S(1)} %multiply_add_fusion.3), channel_id=1, source_target_pairs={{0,16},{16,32},{32,48},{48,64},{64,80},{80,96},{96,112},{112,128},... | collective-permute-start | bytes 98312 | tf_op jit(solution)/shard_map/while/body/eval_jaxpr/ppermute | solution.py:16
  299.5 6.8 %collective-permute-start = (f32[512,16]{0,1:T(8,128)S(1)}, f32[512,16]{0,1:T(8,128)S(1)}, u32[]{:S(2)}, u32[]{:S(2)}) collective-permute-start(f32[512,16]{0,1:T(8,128)S(1)} %multiply_add_fusion.3), channel_id=1, source_target_pairs={{0,16},{16,32},{32,48},{48,64},{64,80},{80,96},{96,112},{112,128},... | collective-permute-start | bytes 98312 | tf_op jit(solution)/shard_map/while/body/eval_jaxpr/ppermute | solution.py:16
  306.3 6.8 %collective-permute-start = (f32[512,16]{0,1:T(8,128)S(1)}, f32[512,16]{0,1:T(8,128)S(1)}, u32[]{:S(2)}, u32[]{:S(2)}) collective-permute-start(f32[512,16]{0,1:T(8,128)S(1)} %multiply_add_fusion.3), channel_id=1, source_target_pairs={{0,16},{16,32},{32,48},{48,64},{64,80},{80,96},{96,112},{112,128},... | collective-permute-start | bytes 98312 | tf_op jit(solution)/shard_map/while/body/eval_jaxpr/ppermute | solution.py:16
  313.0 6.9 %collective-permute-start = (f32[512,16]{0,1:T(8,128)S(1)}, f32[512,16]{0,1:T(8,128)S(1)}, u32[]{:S(2)}, u32[]{:S(2)}) collective-permute-start(f32[512,16]{0,1:T(8,128)S(1)} %multiply_add_fusion.3), channel_id=1, source_target_pairs={{0,16},{16,32},{32,48},{48,64},{64,80},{80,96},{96,112},{112,128},... | collective-permute-start | bytes 98312 | tf_op jit(solution)/shard_map/while/body/eval_jaxpr/ppermute | solution.py:16
  324.4 153.3 %all-gather.15.cloned.1.call-start = ((), (), s32[]{:S(2)}) async-start(), calls=%async_computation.9 | async-start | bytes 4456448 | tf_op jit(solution)/shard_map/all_gather | solution.py:138
  424.3 150.5 %reduce-scatter.5.cloned.1.call-start = ((), (), s32[]{:S(2)}) async-start(), calls=%async_computation.10 | async-start | bytes 4456448 | tf_op jit(solution)/shard_map/reduce_scatter | solution.py:147
  576.6 21.1 %all-to-all-start.1 = ((bf16[16,2,4096]{2,1,0:T(2,128)(2,1)}), bf16[16,2,4096]{2,1,0:T(2,128)(2,1)S(1)}, u32[]{:S(2)}, u32[]{:S(2)}) async-start(bf16[16,2,4096]{2,1,0:T(2,128)(2,1)} %reshape.76), calls=%async_computation.3 | async-start | bytes 524288 | tf_op jit(solution)/shard_map/all_to_all | solution.py:150
  (7 other events, 1031.3 us)
Sparse Core Ops, SparseCore 0:
  9.1 41.8 all-gather.6
  53.4 55.2 all-gather.8
  111.1 56.2 all-gather.10
  169.7 61.4 all-gather.12
  324.5 78.3 reduce-scatter.2
  424.5 53.1 all-gather.14
  494.0 80.7 reduce-scatter.4
